TPU v7x, 512 devices: a whole 4x4x16 slice. The times are simulated.
512 devices in a mesh: blk: 32 (over y, x, core), mpo: 16 (over z).
Axes of the slice: x: 4, y: 4, z: 16, core: 2. Of those that a mesh axis runs over, the one named last changes fastest.
Arguments:
- theta: float32 [64, 128, 16, 128], P('blk'), may hold values from -6 to 6
- block_dims: int32 [64, 2], P('blk'), may hold values from 32 to 128, as said below
- pair_mask: int32 [96, 64], P(None, 'blk'), may hold values 0 or 1
- term_charge: int32 [96], replicated, may hold values from -1 to 1
- left_env: float32 [96, 64, 128, 128], P('mpo', 'blk'), may hold values from -0.5 to 0.5
- right_env: float32 [96, 64, 128, 128], P('mpo', 'blk'), may hold values from -0.5 to 0.5
- site_one: float32 [96, 4, 4], replicated, may hold values from -0.3125 to 0.3125
- site_two: float32 [96, 4, 4], replicated, may hold values from -3 to 3
Outputs:
- hpsi: float32 [64, 128, 16, 128], P('blk', 'mpo')
Inputs may be any that keep to these rules, and one draw needn't show every extreme that they name: `block_dims`: kept dimensions of each sector; rows and columns of a block beyond them are empty. The first sector keeps 128 on both sides.
All inputs are finite; a program needn't handle non-finite values. No bound on the sum of `pair_mask` on one device may be relied on, other than what follows from the above.
Results may differ from a plain program's by a relative error of at most 0.0003.
Values sent between devices are 32-bit elements; how exact they have to be, the bound alone decides.
A program may use at most 64 MiB of HBM per device.

v0:
```python
import jax
import jax.numpy as jnp
from jax import lax
from jax.sharding import PartitionSpec as P


def extended(cells, sides, width):
    for axis, dim in sides:
        count = lax.axis_size(axis)
        ends = count - 1
        head = lax.slice_in_dim(cells, 0, width, axis=dim)
        tail = lax.slice_in_dim(cells, cells.shape[dim] - width, cells.shape[dim], axis=dim)
        cells = jnp.concatenate(
            [
                lax.ppermute(tail, axis, [(i, (i + 1) % count) for i in range(ends)]),
                cells,
                lax.ppermute(head, axis, [((i + 1) % count, i) for i in range(ends)]),
            ],
            axis=dim,
        )
    return cells


def sector_mask(block_dims, bond_cap):
    positions = jnp.arange(bond_cap, dtype=jnp.int32)
    left_ok = positions[None, :] < block_dims[:, 0:1]
    right_ok = positions[None, :] < block_dims[:, 1:2]
    return (left_ok[:, :, None] & right_ok[:, None, :]).astype(jnp.float32)


def make_pair(first_op, second_op):
    states = first_op.shape[0]
    return (first_op[:, None, :, None] * second_op[None, :, None, :]).reshape(
        states * states, states * states
    )


def apply_term(left_rows, source, site_pair, right_block):
    highest = lax.Precision.HIGHEST
    row_count = left_rows.shape[0]
    moved = jnp.dot(
        left_rows,
        source.reshape(source.shape[0], -1),
        precision=highest,
        preferred_element_type=jnp.float32,
    )
    moved = moved.reshape(row_count, source.shape[1], source.shape[2])
    mixed = jnp.einsum("pq,aqd->apd", site_pair, moved, precision=highest)
    return jnp.einsum("apd,bd->apb", mixed, right_block, precision=highest)


def all_sectors(running, padded, left_all, right_all, charge, site_pair, allowed):
    sectors = left_all.shape[0]
    source_index = jnp.arange(sectors, dtype=jnp.int32) + 1 - charge

    def per_sector(left_rows, index, right_block):
        source = lax.dynamic_index_in_dim(padded, index, 0, keepdims=False)
        return apply_term(left_rows, source, site_pair, right_block)

    terms = jax.vmap(per_sector)(left_all, source_index, right_all)
    return running + allowed.astype(jnp.float32)[:, None, None, None] * terms


def body(theta, block_dims, pair_mask, term_charge, left_env, right_env, site_one, site_two):
    bond_cap = theta.shape[1]
    group_index = lax.axis_index("mpo")
    group_count = lax.axis_size("mpo")
    row_count = bond_cap // group_count
    first_row = group_index * row_count
    block_mask = sector_mask(block_dims, bond_cap)
    masked = theta * block_mask[:, :, None, :]
    padded = extended(masked, (("blk", 0),), 1)
    row_mask = lax.dynamic_slice_in_dim(block_mask, first_row, row_count, 1)
    term_count = left_env.shape[0]
    first_term = group_index * term_count

    def local_term(w, running):
        term_index = first_term + w
        charge = lax.dynamic_index_in_dim(term_charge, term_index, 0, keepdims=False)
        allowed = lax.dynamic_index_in_dim(pair_mask, term_index, 0, keepdims=False)
        first_op = lax.dynamic_index_in_dim(site_one, term_index, 0, keepdims=False)
        second_op = lax.dynamic_index_in_dim(site_two, term_index, 0, keepdims=False)
        left_all = lax.dynamic_index_in_dim(left_env, w, 0, keepdims=False)
        right_all = lax.dynamic_index_in_dim(right_env, w, 0, keepdims=False)
        return all_sectors(
            running, padded, left_all, right_all, charge, make_pair(first_op, second_op), allowed
        )

    partial_value = lax.fori_loop(0, term_count, local_term, jnp.zeros(theta.shape, jnp.float32))
    whole_sum = lax.psum(partial_value, "mpo")
    mine = lax.dynamic_slice_in_dim(whole_sum, first_row, row_count, 1)
    return mine * row_mask[:, :, None, :]


def solution(mesh):
    placed = (
        P("blk", None, None, None),
        P("blk", None),
        P(None, "blk"),
        P(),
        P("mpo", "blk", None, None),
        P("mpo", "blk", None, None),
        P(),
        P(),
    )
    return jax.shard_map(
        body, mesh=mesh, in_specs=placed, out_specs=P("blk", "mpo", None, None), check_vma=False
    )
```

profile of v0, /device:TPU:6, one launch (start us, length us, event | category | flops | bytes accessed | tf_op | source)
XLA Modules:
  0.0 307.2 jit_solution(4016067030616916532)
XLA Ops:
  13.1 3.6 %collective-permute-start.1 = (f32[1,128,16,128]{3,1,2,0:T(8,128)S(1)}, f32[1,128,16,128]{3,1,2,0:T(8,128)}, u32[]{:S(2)}, u32[]{:S(2)}) collective-permute-start(f32[1,128,16,128]{3,1,2,0:T(8,128)S(1)} %get-tuple-element.253), channel_id=1, source_target_pairs={{16,0},{32,16},{48,32},{64,48},{80,64},{96,80},{112,96},{128,112},... | collective-permute-start | bytes 3145736 | tf_op jit(solution)/shard_map/ppermute | solution.py:17
  17.8 9.7 %collective-permute-done = f32[1,128,16,128]{3,1,2,0:T(8,128)} collective-permute-done((f32[1,128,16,128]{3,1,2,0:T(8,128)}, f32[1,128,16,128]{3,1,2,0:T(8,128)}, u32[]{:S(2)}, u32[]{:S(2)}) %collective-permute-start) | collective-permute-done | bytes 1048608 | tf_op jit(solution)/shard_map/ppermute | solution.py:15
  29.0 4.0 %pad_maximum_fusion = f32[4,128,16,128]{3,1,2,0:T(8,128)} fusion(f32[1,128,16,128]{3,1,2,0:T(8,128)} %collective-permute-done.1, f32[2,128,16,128]{3,1,2,0:T(8,128)S(1)} %copy_multiply_fusion, f32[1,128,16,128]{3,1,2,0:T(8,128)} %collective-permute-done), kind=kLoop, calls=%fused_computation.25 | loop fusion | flops 2097152 | bytes 8388608 | tf_op jit(solution)/shard_map/concatenate | solution.py:13
  33.0 109.8 %while.14 = (s32[]{:T(128)}, f32[2,128,16,128]{3,1,2,0:T(8,128)}, s32[]{:T(128)}, s32[96,2]{1,0:T(8,128)S(1)}, f32[6,2,128,128]{3,2,1,0:T(8,128)}, /*index=5*/s3...) while((s32[]{:T(128)}, f32[2,128,16,128]{3,1,2,0:T(8,128)}, ...), condition=%wide.region_1.2_spmd.clone, body=%wide.region_0.1_spmd.clone.sunk | while | flops 1712849152 | bytes 44307156 | solution.py:89
  35.0 2.9 gather_fusion
  39.7 3.6 %fusion.37 = f32[2,128,2048]{2,1,0:T(8,128)S(1)} fusion(f32[2,128,2048]{1,2,0:T(8,128)} %bitcast.61, f32[6,2,128,128]{3,2,1,0:T(8,128)} %get-tuple-element.351, s32[]{:T(128)S(6)} %copy.41), kind=kOutput, calls=%fused_computation.8.clone.1 | convolution fusion | flops 805306368 | bytes 4325380 | tf_op jit(solution)/shard_map/while/body/eval_jaxpr/vmap()/dot_general | solution.py:41
  45.6 4.4 %select_add_fusion.2 = f32[2,128,16,128]{3,1,2,0:T(8,128)S(1)} fusion(f32[2,128,16,128]{3,1,2,0:T(8,128)S(1)} %copy-done, f32[2,128,128,16]{2,3,1,0:T(8,128)S(1)} %fusion.38, f32[2]{0:T(128)S(1)} %fusion.39, pred[]{:T(512)S(6)} %compare.3, f32[6,2,128,128]{3,2,1,0:T(8,128)} %get-tuple-element.356, s32[]{:T(128)S(6)} %copy.41), kind=kOutput, calls=%fused_computation.6.clone.1 | convolution fusion | flops 806879232 | bytes 6422541 | tf_op jit(solution)/shard_map/while/body/eval_jaxpr/vmap(apd,bd->apb)/dot_general | solution.py:49
  53.3 2.9 gather_fusion
  58.0 3.6 %fusion.37 = f32[2,128,2048]{2,1,0:T(8,128)S(1)} fusion(f32[2,128,2048]{1,2,0:T(8,128)} %bitcast.61, f32[6,2,128,128]{3,2,1,0:T(8,128)} %get-tuple-element.351, s32[]{:T(128)S(6)} %copy.41), kind=kOutput, calls=%fused_computation.8.clone.1 | convolution fusion | flops 805306368 | bytes 4325380 | tf_op jit(solution)/shard_map/while/body/eval_jaxpr/vmap()/dot_general | solution.py:41
  63.9 4.4 %select_add_fusion.2 = f32[2,128,16,128]{3,1,2,0:T(8,128)S(1)} fusion(f32[2,128,16,128]{3,1,2,0:T(8,128)S(1)} %copy-done, f32[2,128,128,16]{2,3,1,0:T(8,128)S(1)} %fusion.38, f32[2]{0:T(128)S(1)} %fusion.39, pred[]{:T(512)S(6)} %compare.3, f32[6,2,128,128]{3,2,1,0:T(8,128)} %get-tuple-element.356, s32[]{:T(128)S(6)} %copy.41), kind=kOutput, calls=%fused_computation.6.clone.1 | convolution fusion | flops 806879232 | bytes 6422541 | tf_op jit(solution)/shard_map/while/body/eval_jaxpr/vmap(apd,bd->apb)/dot_general | solution.py:49
  71.6 2.9 gather_fusion
  76.3 3.6 %fusion.37 = f32[2,128,2048]{2,1,0:T(8,128)S(1)} fusion(f32[2,128,2048]{1,2,0:T(8,128)} %bitcast.61, f32[6,2,128,128]{3,2,1,0:T(8,128)} %get-tuple-element.351, s32[]{:T(128)S(6)} %copy.41), kind=kOutput, calls=%fused_computation.8.clone.1 | convolution fusion | flops 805306368 | bytes 4325380 | tf_op jit(solution)/shard_map/while/body/eval_jaxpr/vmap()/dot_general | solution.py:41
  82.2 4.4 %select_add_fusion.2 = f32[2,128,16,128]{3,1,2,0:T(8,128)S(1)} fusion(f32[2,128,16,128]{3,1,2,0:T(8,128)S(1)} %copy-done, f32[2,128,128,16]{2,3,1,0:T(8,128)S(1)} %fusion.38, f32[2]{0:T(128)S(1)} %fusion.39, pred[]{:T(512)S(6)} %compare.3, f32[6,2,128,128]{3,2,1,0:T(8,128)} %get-tuple-element.356, s32[]{:T(128)S(6)} %copy.41), kind=kOutput, calls=%fused_computation.6.clone.1 | convolution fusion | flops 806879232 | bytes 6422541 | tf_op jit(solution)/shard_map/while/body/eval_jaxpr/vmap(apd,bd->apb)/dot_general | solution.py:49
  89.9 2.9 gather_fusion
  94.6 3.6 %fusion.37 = f32[2,128,2048]{2,1,0:T(8,128)S(1)} fusion(f32[2,128,2048]{1,2,0:T(8,128)} %bitcast.61, f32[6,2,128,128]{3,2,1,0:T(8,128)} %get-tuple-element.351, s32[]{:T(128)S(6)} %copy.41), kind=kOutput, calls=%fused_computation.8.clone.1 | convolution fusion | flops 805306368 | bytes 4325380 | tf_op jit(solution)/shard_map/while/body/eval_jaxpr/vmap()/dot_general | solution.py:41
  100.5 4.4 %select_add_fusion.2 = f32[2,128,16,128]{3,1,2,0:T(8,128)S(1)} fusion(f32[2,128,16,128]{3,1,2,0:T(8,128)S(1)} %copy-done, f32[2,128,128,16]{2,3,1,0:T(8,128)S(1)} %fusion.38, f32[2]{0:T(128)S(1)} %fusion.39, pred[]{:T(512)S(6)} %compare.3, f32[6,2,128,128]{3,2,1,0:T(8,128)} %get-tuple-element.356, s32[]{:T(128)S(6)} %copy.41), kind=kOutput, calls=%fused_computation.6.clone.1 | convolution fusion | flops 806879232 | bytes 6422541 | tf_op jit(solution)/shard_map/while/body/eval_jaxpr/vmap(apd,bd->apb)/dot_general | solution.py:49
  108.2 2.9 gather_fusion
  112.9 3.6 %fusion.37 = f32[2,128,2048]{2,1,0:T(8,128)S(1)} fusion(f32[2,128,2048]{1,2,0:T(8,128)} %bitcast.61, f32[6,2,128,128]{3,2,1,0:T(8,128)} %get-tuple-element.351, s32[]{:T(128)S(6)} %copy.41), kind=kOutput, calls=%fused_computation.8.clone.1 | convolution fusion | flops 805306368 | bytes 4325380 | tf_op jit(solution)/shard_map/while/body/eval_jaxpr/vmap()/dot_general | solution.py:41
  118.8 4.4 %select_add_fusion.2 = f32[2,128,16,128]{3,1,2,0:T(8,128)S(1)} fusion(f32[2,128,16,128]{3,1,2,0:T(8,128)S(1)} %copy-done, f32[2,128,128,16]{2,3,1,0:T(8,128)S(1)} %fusion.38, f32[2]{0:T(128)S(1)} %fusion.39, pred[]{:T(512)S(6)} %compare.3, f32[6,2,128,128]{3,2,1,0:T(8,128)} %get-tuple-element.356, s32[]{:T(128)S(6)} %copy.41), kind=kOutput, calls=%fused_computation.6.clone.1 | convolution fusion | flops 806879232 | bytes 6422541 | tf_op jit(solution)/shard_map/while/body/eval_jaxpr/vmap(apd,bd->apb)/dot_general | solution.py:49
  126.5 2.9 gather_fusion
  131.2 3.6 %fusion.37 = f32[2,128,2048]{2,1,0:T(8,128)S(1)} fusion(f32[2,128,2048]{1,2,0:T(8,128)} %bitcast.61, f32[6,2,128,128]{3,2,1,0:T(8,128)} %get-tuple-element.351, s32[]{:T(128)S(6)} %copy.41), kind=kOutput, calls=%fused_computation.8.clone.1 | convolution fusion | flops 805306368 | bytes 4325380 | tf_op jit(solution)/shard_map/while/body/eval_jaxpr/vmap()/dot_general | solution.py:41
  137.1 4.4 %select_add_fusion.2 = f32[2,128,16,128]{3,1,2,0:T(8,128)S(1)} fusion(f32[2,128,16,128]{3,1,2,0:T(8,128)S(1)} %copy-done, f32[2,128,128,16]{2,3,1,0:T(8,128)S(1)} %fusion.38, f32[2]{0:T(128)S(1)} %fusion.39, pred[]{:T(512)S(6)} %compare.3, f32[6,2,128,128]{3,2,1,0:T(8,128)} %get-tuple-element.356, s32[]{:T(128)S(6)} %copy.41), kind=kOutput, calls=%fused_computation.6.clone.1 | convolution fusion | flops 806879232 | bytes 6422541 | tf_op jit(solution)/shard_map/while/body/eval_jaxpr/vmap(apd,bd->apb)/dot_general | solution.py:49
  142.8 4.2 %copy.20 = f32[2,128,16,128]{3,2,1,0:T(8,128)} copy(f32[2,128,16,128]{3,1,2,0:T(8,128)} %get-tuple-element.174) | data formatting | bytes 4194304 | tf_op jit(solution)/shard_map/while | solution.py:89
  147.0 151.8 %all-reduce.2.cloned.1.call-done = f32[2,128,16,128]{3,2,1,0:T(8,128)} async-done(((f32[2,128,16,128]{3,2,1,0:T(8,128)}), f32[2,128,16,128]{3,2,1,0:T(8,128)}) %all-reduce.2.cloned.1.call-update) | async-done | bytes 2097168 | tf_op jit(solution)/shard_map/psum | solution.py:90
  (101 shorter events, 55.1 us)
Async XLA Ops:
  6.5 292.2 %all-reduce.2.cloned.1.call-start = ((), (), s32[]{:S(2)}) async-start(), calls=%async_computation | async-start | bytes 4194304 | tf_op jit(solution)/shard_map/psum | solution.py:90
  9.9 6.8 %copy-start.4 = (s32[96,2]{0,1:T(2,128)S(1)}, s32[96,2]{0,1:T(2,128)}, u32[]{:S(2)}) copy-start(s32[96,2]{0,1:T(2,128)} %param.12) | copy-start | bytes 2308
  10.0 6.9 %copy-start.2 = (f32[96,4,4]{0,2,1:T(4,128)S(1)}, f32[96,4,4]{0,2,1:T(4,128)}, u32[]{:S(2)}) copy-start(f32[96,4,4]{0,2,1:T(4,128)} %param.16) | copy-start | bytes 18436
  10.0 7.0 %copy-start.3 = (f32[96,4,4]{0,2,1:T(4,128)S(1)}, f32[96,4,4]{0,2,1:T(4,128)}, u32[]{:S(2)}) copy-start(f32[96,4,4]{0,2,1:T(4,128)} %param.17) | copy-start | bytes 18436
  11.1 16.4 %collective-permute-start = (f32[1,128,16,128]{3,1,2,0:T(8,128)}, f32[1,128,16,128]{3,1,2,0:T(8,128)}, u32[]{:S(2)}, u32[]{:S(2)}) collective-permute-start(f32[1,128,16,128]{3,1,2,0:T(8,128)} %get-tuple-element.252), channel_id=1, source_target_pairs={{0,16},{16,32},{32,48},{48,64},{64,80},{80,96},{96,112},{112,128},... | collective-permute-start | bytes 3145736 | tf_op jit(solution)/shard_map/ppermute | solution.py:15
  13.1 15.9 %collective-permute-start.1 = (f32[1,128,16,128]{3,1,2,0:T(8,128)S(1)}, f32[1,128,16,128]{3,1,2,0:T(8,128)}, u32[]{:S(2)}, u32[]{:S(2)}) collective-permute-start(f32[1,128,16,128]{3,1,2,0:T(8,128)S(1)} %get-tuple-element.253), channel_id=1, source_target_pairs={{16,0},{32,16},{48,32},{64,48},{80,64},{96,80},{112,96},{128,112},... | collective-permute-start | bytes 3145736 | tf_op jit(solution)/shard_map/ppermute | solution.py:17
  17.8 15.1 %copy-start.5 = (s32[96]{0:T(128)S(1)}, s32[96]{0:T(128)}, u32[]{:S(2)}) copy-start(s32[96]{0:T(128)} %param.13) | copy-start | bytes 1156
  43.7 1.9 copy-start
  49.9 1.3 copy-start.1
  62.0 1.9 copy-start
  68.3 1.3 copy-start.1
  80.3 1.9 copy-start
  86.6 1.3 copy-start.1
  98.6 1.9 copy-start
  104.9 1.3 copy-start.1
  116.9 1.9 copy-start
  123.2 1.3 copy-start.1
  135.2 1.9 copy-start
  141.5 1.3 copy-start.1
Sparse Core Ops, SparseCore 0:
  147.1 151.6 all-reduce.1
where the time goes:
time: 308 us; the launch traced here: 307 us
  waiting for transfers between devices  163 us (53%)
  matrix products  58.9 us (19%)
  local copies, waits for them, and re-layouts  53.9 us (18%)
  between operations  13.5 us (4%)
  other arithmetic  11.8 us (4%)
  starting transfers between devices  5.55 us (2%)
    psum x1, waiting for transfers between devices, body(): whole_sum = lax.psum(partial_value, 'mpo')  152 us
    gather x12, local copies, waits for them, and re-layouts, per_sector(): source = lax.dynamic_index_in_dim(padded, index, 0, keepdims=False)  28.4 us
    dot_general x6, matrix products, apply_term(): return jnp.einsum('apd,bd->apb', mixed, right_block, precision=highest)  26.2 us
    dot_general x6, matrix products, apply_term(): jnp.dot(left_rows, source.reshape(source.shape[0], -1), precision=highest...  21.4 us
    dot_general x6, matrix products, apply_term(): mixed = jnp.einsum('pq,aqd->apd', site_pair, moved, precision=highest)  11.3 us
    while x30, local copies, waits for them, and re-layouts  10.3 us
    ppermute x1, waiting for transfers between devices, extended(): lax.ppermute(tail, axis, [(i, (i + 1) % count) for i in range(ends)])  9.72 us
  transfers between devices with their start and end apart: 3, of which 3 were waited for; matrix products, arithmetic and copies ran while one was open for 0% of the time, Pallas kernels for 0%

commit v1 on v0

v1 whole, which is shorter than its diff:
```python
import functools

import jax
import jax.numpy as jnp
from jax import lax
from jax.experimental import pallas as pl
from jax.experimental.pallas import tpu as pltpu
from jax.sharding import PartitionSpec as P

MESH = pl.DeviceIdType.MESH
F32 = jnp.float32
BF16 = jnp.bfloat16
CB = 32


def halves(x):
    high = x.astype(BF16)
    return high, (x - high.astype(F32)).astype(BF16)


def kernel(
    theta, left, right, dims_v, dims_s, charge, pair, one, two,
    out,
    theta_v, halo_v, left_v, right_v, dims_halo, dims_all, split, mixed, rows, part, arrived,
    local_sem, halo_send, halo_recv, ring_send, ring_recv,
):
    terms, _, cap, _ = left.shape
    site = one.shape[1]
    pairs = site * site
    n_blk, n = lax.axis_size("blk"), lax.axis_size("mpo")
    half = n // 2
    rc = cap // n
    blk, me = lax.axis_index("blk"), lax.axis_index("mpo")
    next_blk, last_blk = lax.rem(blk + 1, n_blk), lax.rem(blk + n_blk - 1, n_blk)
    up, down = lax.rem(me + 1, n), lax.rem(me + n - 1, n)
    w0 = me * terms

    local = [
        pltpu.make_async_copy(theta, theta_v, local_sem.at[0]),
        pltpu.make_async_copy(left, left_v, local_sem.at[1]),
        pltpu.make_async_copy(right, right_v, local_sem.at[2]),
    ]
    for copy in local:
        copy.start()

    barrier = pltpu.get_barrier_semaphore()
    for target in ({"blk": next_blk}, {"blk": last_blk}, {"mpo": up}, {"mpo": down}):
        pl.semaphore_signal(barrier, inc=1, device_id=target, device_id_type=MESH)
    pl.semaphore_wait(barrier, 4)

    def halo_copy(side, src, dst, index):
        return pltpu.make_async_remote_copy(
            src_ref=src.at[1 - side], dst_ref=dst.at[side],
            send_sem=halo_send.at[index, side], recv_sem=halo_recv.at[index, side],
            device_id={"blk": next_blk if side == 0 else last_blk}, device_id_type=MESH,
        )

    halo = [halo_copy(side, dims_v, dims_halo, 0) for side in (0, 1)]
    halo += [halo_copy(side, theta, halo_v, 1) for side in (0, 1)]
    for copy in halo:
        copy.start()

    def prepare(source, block_ref, index):
        def body(cb, carry):
            for q in range(pairs):
                start = cb * (CB * pairs) + q
                high, low = halves(block_ref[index, pl.ds(start, CB, stride=pairs), :])
                split[source, cb, pl.ds(q * CB, CB), pl.ds(0, cap)] = high
                split[source, cb, pl.ds(q * CB, CB), pl.ds(cap, cap)] = low
            return carry

        lax.fori_loop(0, cap // CB, body, 0)

    lane = lax.broadcasted_iota(jnp.int32, (8, cap), 1).astype(F32)[0:1]

    def apply_right(slot, w, k, source):
        row = dims_all[source]
        weight = jnp.where(lane < row[1:2], right_v[w, k], 0.0)
        high, low = halves(weight)
        weights = jnp.concatenate(
            [
                jnp.concatenate([high, high], axis=1),
                jnp.concatenate([low, jnp.zeros_like(low)], axis=1),
            ],
            axis=0,
        )
        allowed = pair[w0 + w, k].astype(F32)
        first = [[one[w0 + w, s, t] * allowed for t in range(site)] for s in range(site)]
        second = [[two[w0 + w, u, v] for v in range(site)] for u in range(site)]
        def step(cb, carry):
            both = lax.dot_general(
                split[source, cb], weights, (((1,), (1,)), ((), ())), preferred_element_type=F32
            )
            y = both[:, :cap] + both[:, cap:]
            y = [y[q * CB:(q + 1) * CB] for q in range(pairs)]
            z = [
                [sum(second[u][v] * y[t * site + v] for v in range(site)) for u in range(site)]
                for t in range(site)
            ]
            for s in range(site):
                for u in range(site):
                    p = s * site + u
                    m_high, m_low = halves(sum(first[s][t] * z[t][u] for t in range(site)))
                    start = pl.multiple_of(cb * CB, CB)
                    mixed[slot, pl.ds(start, CB), pl.ds(p * cap, cap)] = m_high
                    mixed[slot, pl.ds(cap + start, CB), pl.ds(p * cap, cap)] = m_low
            return carry

        lax.fori_loop(0, cap // CB, step, 0)

    local[0].wait()
    local[2].wait()
    dims_all[1] = dims_v[0]
    dims_all[2] = dims_v[1]
    for k in range(2):
        prepare(1 + k, theta_v, k)

    def near(w, carry):
        q = charge[w0 + w]
        k = jnp.where(q == 1, 1, 0)
        apply_right(w, w, k, k + 1 - q)
        return carry

    lax.fori_loop(0, terms, near, 0)

    for copy in halo:
        copy.wait()
    for side, source in ((0, 0), (1, 3)):
        outside = blk == (0 if side == 0 else n_blk - 1)
        dims_all[source] = dims_halo[side] * jnp.where(outside, 0.0, 1.0)
        prepare(source, halo_v, side)

    def far(w, carry):
        q = charge[w0 + w]
        k = jnp.where(q == 1, 0, 1)
        apply_right(terms + w, w, k, k + 1 - q)
        return carry

    lax.fori_loop(0, terms, far, 0)

    local[1].wait()

    def rotate(g, carry):
        ahead = pl.multiple_of(lax.rem(me + half - g, n) * rc, rc)
        behind = pl.multiple_of(jnp.where(g == 0, me, lax.rem(me + n - half + g, n)) * rc, rc)
        for w in range(terms):
            q = charge[w0 + w]
            for k in range(2):
                row = dims_all[k + 1 - q]
                block = jnp.concatenate(
                    [left_v[w, k, pl.ds(ahead, rc), :], left_v[w, k, pl.ds(behind, rc), :]], axis=0
                )
                high, low = halves(jnp.where(lane < row[0:1], block, 0.0))
                rows[g, k, w] = jnp.concatenate(
                    [
                        jnp.concatenate([high, high], axis=1),
                        jnp.concatenate([low, jnp.zeros_like(low)], axis=1),
                    ],
                    axis=0,
                )
        return carry

    lax.fori_loop(0, half, rotate, 0)

    wide = 4 * cap

    def compute(g):
        for k in range(2):

            def columns(c, carry):
                start = pl.multiple_of(c * wide, wide)
                total = jnp.zeros((4 * rc, wide), F32)
                for w in range(terms):
                    q = charge[w0 + w]
                    slot = w + jnp.where((q == 1) == (k == 1), 0, terms)
                    total += jnp.dot(
                        rows[g, k, w], mixed[slot, :, pl.ds(start, wide)], preferred_element_type=F32
                    )
                total = total[:2 * rc] + total[2 * rc:]
                part[g, 0, k, :, pl.ds(start, wide)] = total[:rc]
                part[g, 1, k, :, pl.ds(start, wide)] = total[rc:]
                return carry

            lax.fori_loop(0, pairs * cap // wide, columns, 0)

    def ring_copy(step, way, k):
        return pltpu.make_async_remote_copy(
            src_ref=part.at[step, 0 if isinstance(step, int) and step == 0 else way, k], dst_ref=arrived.at[step, way, k],
            send_sem=ring_send.at[step, way, k], recv_sem=ring_recv.at[step, way, k],
            device_id={"mpo": up if way == 0 else down}, device_id_type=MESH,
        )

    def ring_step(step, first):
        for k in range(2):
            for way in range(2):
                if first and k != way:
                    ring_copy(step, way, k).start()
        for k in range(2):
            for way in range(2):
                if not first or k == way:
                    ring_copy(step - 1, way, k).wait_recv()
                    part[step, way, k] += arrived[step - 1, way, k]
                    ring_copy(step, way, k).start()

    compute(0)
    for way in range(2):
        ring_copy(0, way, way).start()
    compute(1)
    ring_step(1, True)

    def later(step, carry):
        compute(step)
        ring_step(step, False)
        return carry

    lax.fori_loop(2, half, later, 0)

    for k in range(2):
        total = part[0, 1, k]
        for way in range(2):
            ring_copy(half - 1, way, k).wait_recv()
            total = total + arrived[half - 1, way, k]
        row = lax.broadcasted_iota(jnp.int32, (rc, cap), 0) + me * rc
        column = lax.broadcasted_iota(jnp.int32, (rc, cap), 1)
        keep = (row < dims_s[k, 0]) & (column < dims_s[k, 1])
        for p in range(pairs):
            out[k, :, p, :] = jnp.where(keep, total[:, p * cap:(p + 1) * cap], 0.0)

    for way in range(2):
        ring_copy(0, way, way).wait_send()

    def drain(step, carry):
        for way in range(2):
            for k in range(2):
                ring_copy(step, way, k).wait_send()
        return carry

    lax.fori_loop(1, half, drain, 0)


def body(theta, block_dims, pair_mask, term_charge, left_env, right_env, site_one, site_two):
    sectors, cap, pairs, _ = theta.shape
    terms = left_env.shape[0]
    half = lax.axis_size("mpo") // 2
    rc = cap // (2 * half)
    dims_v = jnp.broadcast_to(
        jnp.pad(block_dims.astype(F32), ((0, 0), (0, 6)))[:, :, None], (sectors, 8, cap)
    )
    anywhere = pl.BlockSpec(memory_space=pl.ANY)
    vmem = pl.BlockSpec(memory_space=pltpu.VMEM)
    smem = pl.BlockSpec(memory_space=pltpu.SMEM)
    return pl.pallas_call(
        kernel,
        out_shape=jax.ShapeDtypeStruct((sectors, rc, pairs, cap), F32),
        in_specs=[anywhere] * 3 + [vmem] + [smem] * 5,
        out_specs=vmem,
        scratch_shapes=[
            pltpu.VMEM((sectors, cap * pairs, cap), F32),
            pltpu.VMEM((2, cap * pairs, cap), F32),
            pltpu.VMEM(left_env.shape, F32),
            pltpu.VMEM(right_env.shape, F32),
            pltpu.VMEM((2, 8, cap), F32),
            pltpu.VMEM((4, 8, cap), F32),
            pltpu.VMEM((4, cap // CB, pairs * CB, 2 * cap), BF16),
            pltpu.VMEM((2 * terms, 2 * cap, pairs * cap), BF16),
            pltpu.VMEM((half, 2, terms, 4 * rc, 2 * cap), BF16),
            pltpu.VMEM((half, 2, 2, rc, pairs * cap), F32),
            pltpu.VMEM((half, 2, 2, rc, pairs * cap), F32),
            pltpu.SemaphoreType.DMA((3,)),
            pltpu.SemaphoreType.DMA((2, 2)),
            pltpu.SemaphoreType.DMA((2, 2)),
            pltpu.SemaphoreType.DMA((half, 2, 2)),
            pltpu.SemaphoreType.DMA((half, 2, 2)),
        ],
        compiler_params=pltpu.CompilerParams(
            collective_id=0, has_side_effects=True, vmem_limit_bytes=60 * 2**20
        ),
    )(
        theta.reshape(sectors, cap * pairs, cap), left_env, right_env, dims_v, block_dims, term_charge,
        pair_mask, site_one, site_two,
    )


def solution(mesh):
    placed = (
        P("blk", None, None, None),
        P("blk", None),
        P(None, "blk"),
        P(),
        P("mpo", "blk", None, None),
        P("mpo", "blk", None, None),
        P(),
        P(),
    )
    return jax.shard_map(
        body, mesh=mesh, in_specs=placed, out_specs=P("blk", "mpo", None, None), check_vma=False
    )
```

time: 308 us -> 89.4 us (0.29)
  the two profiles are of different devices: /device:TPU:6 before, /device:TPU:16 now
where the time goes in v1:
time: 89.4 us; the launch traced here: 89.2 us
  Pallas kernels  81.8 us (91%)
  local copies, waits for them, and re-layouts  6.64 us (7%)
    pallas_call x1, Pallas kernels, body(): pl.pallas_call(kernel, out_shape=jax.ShapeDtypeStruct((sectors, rc, pairs...  81.8 us
    unnamed x4, local copies, waits for them, and re-layouts  5.97 us

profile of v1, /device:TPU:16, one launch (start us, length us, event | category | flops | bytes accessed | tf_op | source)
XLA Modules:
  0.0 89.2 jit_solution(1048769550142206618)
XLA Ops:
  0.0 0.7 convert_element_type.5
  0.7 0.7 broadcast_in_dim.2.dims_v
  1.4 1.4 %copy.9.pair = s32[96,2]{1,0:T(8,128)} copy(s32[96,2]{0,1:T(2,128)} %param.10) | data formatting | bytes 1536 | tf_op args[2]
  2.8 1.5 %copy.10.one = f32[96,4,4]{2,1,0:T(4,128)} copy(f32[96,4,4]{0,2,1:T(4,128)} %param.14) | data formatting | bytes 12288 | tf_op args[6]
  4.3 1.5 %copy.11.two = f32[96,4,4]{2,1,0:T(4,128)} copy(f32[96,4,4]{0,2,1:T(4,128)} %param.15) | data formatting | bytes 12288 | tf_op args[7]
  5.8 81.8 %shard_map.82 = f32[2,8,16,128]{3,2,1,0:T(8,128)} custom-call(f32[2,2048,128]{2,1,0:T(8,128)} %bitcast.1, f32[6,2,128,128]{3,2,1,0:T(8,128)} %left.1, f32[6,2,128,128]{3,2,1,0:T(8,128)} %right.1, f32[2,8,128]{2,1,0:T(8,128)} %broadcast_in_dim.2.dims_v, s32[2,2]{1,0:T(2,128)} %dims_s.1, s32[96]{0:T(128)} %charge.1, s32[96,2]{1,0:T(8,128)} %copy.9.pair, ...), custom_call_target="tpu_custom_call" | custom-call | tf_op jit(solution)/shard_map/pallas_call | solution.py:252
  87.6 1.6 %copy.13 = f32[2,8,16,128]{3,2,1,0:T(8,128)} copy(f32[2,8,16,128]{3,2,1,0:T(8,128)} %shard_map.82) | data formatting | bytes 262144
  (1 shorter events, 0.0 us)

commit v2 on v1

v2 whole, which is shorter than its diff:
```python
import functools

import jax
import jax.numpy as jnp
from jax import lax
from jax.experimental import pallas as pl
from jax.experimental.pallas import tpu as pltpu
from jax.sharding import PartitionSpec as P

MESH = pl.DeviceIdType.MESH
F32 = jnp.float32
BF16 = jnp.bfloat16
CB = 32
RB = 16
WIDE = 1024


def halves(x):
    high = x.astype(BF16)
    return high, (x - high.astype(F32)).astype(BF16)


def kernel(
    theta, left, right, dims_s, charge, pair, one, two,
    out,
    theta_v, halo_v, left_v, right_v, dims_v, dims_halo, dims_all, split, weights, mixed, rows, part, arrived,
    local_sem, halo_send, halo_recv, ring_send, ring_recv,
):
    terms, _, cap, _ = left.shape
    site = one.shape[0]
    pairs = site * site
    n_blk, n = lax.axis_size("blk"), lax.axis_size("mpo")
    half = n // 2
    rc = cap // n
    blk, me = lax.axis_index("blk"), lax.axis_index("mpo")
    next_blk, last_blk = lax.rem(blk + 1, n_blk), lax.rem(blk + n_blk - 1, n_blk)
    up, down = lax.rem(me + 1, n), lax.rem(me + n - 1, n)
    w0 = me * terms

    local = [
        pltpu.make_async_copy(theta, theta_v, local_sem.at[0]),
        pltpu.make_async_copy(left, left_v, local_sem.at[1]),
        pltpu.make_async_copy(right, right_v, local_sem.at[2]),
    ]
    for copy in local:
        copy.start()

    for k in range(2):
        top = lax.broadcasted_iota(jnp.int32, (8, cap), 0) == 0
        dims_v[k] = jnp.where(top, dims_s[k, 0], dims_s[k, 1]).astype(F32)

    barrier = pltpu.get_barrier_semaphore()
    for target in ({"blk": next_blk}, {"blk": last_blk}, {"mpo": up}, {"mpo": down}):
        pl.semaphore_signal(barrier, inc=1, device_id=target, device_id_type=MESH)
    pl.semaphore_wait(barrier, 4)

    blocks = cap // CB
    span = CB * pairs

    def halo_copy(side, src, dst, sem):
        return pltpu.make_async_remote_copy(
            src_ref=src, dst_ref=dst, send_sem=halo_send.at[sem, side], recv_sem=halo_recv.at[sem, side],
            device_id={"blk": next_blk if side == 0 else last_blk}, device_id_type=MESH,
        )

    def halo_block(side, cb):
        start = pl.multiple_of(cb * span, span)
        return halo_copy(
            side, theta.at[1 - side, pl.ds(start, span)], halo_v.at[side, pl.ds(start, span)], cb
        )

    halo_dims = [halo_copy(side, dims_v.at[1 - side], dims_halo.at[side], blocks) for side in (0, 1)]
    for copy in halo_dims:
        copy.start()
    for cb in range(blocks):
        for side in (0, 1):
            halo_block(side, cb).start()

    def prepare(source, block_ref, index, cb):
        for q in range(pairs):
            high, low = halves(block_ref[index, pl.ds(cb * span + q, CB, stride=pairs), :])
            split[source, cb, pl.ds(q * CB, CB), pl.ds(0, cap)] = high
            split[source, cb, pl.ds(q * CB, CB), pl.ds(cap, cap)] = low

    lane = lax.broadcasted_iota(jnp.int32, (8, cap), 1).astype(F32)[0:1]

    def weigh(slot, w, k, source):
        row = dims_all[source]
        high, low = halves(jnp.where(lane < row[1:2], right_v[w, k], 0.0))
        weights[slot, pl.ds(0, cap), pl.ds(0, cap)] = high
        weights[slot, pl.ds(0, cap), pl.ds(cap, cap)] = high
        weights[slot, pl.ds(cap, cap), pl.ds(0, cap)] = low
        weights[slot, pl.ds(cap, cap), pl.ds(cap, cap)] = jnp.zeros_like(low)

    def apply_right(slot, w, k, source, cb):
        allowed = pair[k, w0 + w].astype(F32)
        first = [[one[s, t, w0 + w] * allowed for t in range(site)] for s in range(site)]
        second = [[two[u, v, w0 + w] for v in range(site)] for u in range(site)]
        both = lax.dot_general(
            split[source, cb], weights[slot], (((1,), (1,)), ((), ())), preferred_element_type=F32
        )
        for r in range(0, CB, RB):
            z = []
            for t in range(site):
                y = [both[q * CB + r:q * CB + r + RB] for q in range(t * site, (t + 1) * site)]
                y = [block[:, :cap] + block[:, cap:] for block in y]
                z.append([sum(second[u][v] * y[v] for v in range(site)) for u in range(site)])
            start = pl.multiple_of(cb * CB + r, RB)
            for s in range(site):
                for u in range(site):
                    p = s * site + u
                    high, low = halves(sum(first[s][t] * z[t][u] for t in range(site)))
                    mixed[slot, pl.ds(start, RB), pl.ds(p * cap, cap)] = high
                    mixed[slot, pl.ds(cap + start, RB), pl.ds(p * cap, cap)] = low

    def near(w):
        q = charge[w0 + w]
        k = jnp.where(q == 1, 1, 0)
        return w, w, k, k + 1 - q

    def far(w):
        q = charge[w0 + w]
        k = jnp.where(q == 1, 0, 1)
        return terms + w, w, k, k + 1 - q

    def each(count, task):
        lax.fori_loop(0, count, lambda index, carry: (task(index), carry)[1], 0)

    dims_all[1] = dims_v[0]
    dims_all[2] = dims_v[1]
    local[0].wait()
    each(blocks, lambda cb: [prepare(1 + k, theta_v, k, cb) for k in range(2)])
    local[2].wait()
    each(terms, lambda w: weigh(*near(w)))

    def near_term(w):
        each(blocks, lambda cb: apply_right(*near(w), cb))

    each(terms, near_term)

    for side, source in ((0, 0), (1, 3)):
        halo_dims[side].wait()
        outside = blk == (0 if side == 0 else n_blk - 1)
        dims_all[source] = dims_halo[side] * jnp.where(outside, 0.0, 1.0)
    each(terms, lambda w: weigh(*far(w)))

    local[1].wait()

    def rotate(g, carry):
        ahead = pl.multiple_of(lax.rem(me + half - g, n) * rc, rc)
        behind = pl.multiple_of(jnp.where(g == 0, me, lax.rem(me + n - half + g, n)) * rc, rc)
        for w in range(terms):
            q = charge[w0 + w]
            for k in range(2):
                row = dims_all[k + 1 - q]
                block = jnp.concatenate(
                    [left_v[w, k, pl.ds(ahead, rc), :], left_v[w, k, pl.ds(behind, rc), :]], axis=0
                )
                high, low = halves(jnp.where(lane < row[0:1], block, 0.0))
                rows[g, k, w] = jnp.concatenate(
                    [
                        jnp.concatenate([high, high], axis=1),
                        jnp.concatenate([low, jnp.zeros_like(low)], axis=1),
                    ],
                    axis=0,
                )
        return carry

    lax.fori_loop(0, half, rotate, 0)

    def far_block(cb):
        for side, source in ((0, 0), (1, 3)):
            halo_block(side, cb).wait_recv()
            prepare(source, halo_v, side, cb)
        each(terms, lambda w: apply_right(*far(w), cb))

    each(blocks, far_block)

    wide = WIDE
    pieces = pairs * cap // wide

    def columns(c):
        return pl.ds(pl.multiple_of(c * wide, wide), wide)

    def compute(g, k, c):
        total = jnp.zeros((4 * rc, wide), F32)
        for w in range(terms):
            q = charge[w0 + w]
            slot = w + jnp.where((q == 1) == (k == 1), 0, terms)
            total += jnp.dot(
                rows[g, k, w], mixed[slot, :, columns(c)], preferred_element_type=F32
            )
        total = total[:2 * rc] + total[2 * rc:]
        part[g, 0, k, :, columns(c)] = total[:rc]
        part[g, 1, k, :, columns(c)] = total[rc:]

    def ring_copy(step, way, k, c):
        row = 0 if isinstance(step, int) and step == 0 else way
        return pltpu.make_async_remote_copy(
            src_ref=part.at[step, row, k, :, columns(c)], dst_ref=arrived.at[step, way, k, :, columns(c)],
            send_sem=ring_send.at[step, way, k, c], recv_sem=ring_recv.at[step, way, k, c],
            device_id={"mpo": up if way == 0 else down}, device_id_type=MESH,
        )

    def forward(step, way, k, c):
        ring_copy(step - 1, way, k, c).wait_recv()
        part[step, way, k, :, columns(c)] += arrived[step - 1, way, k, :, columns(c)]
        ring_copy(step, way, k, c).start()

    for k in range(2):

        def farthest(c):
            compute(0, k, c)
            ring_copy(0, k, k, c).start()

        each(pieces, farthest)
    for k in range(2):

        def second(c):
            compute(1, k, c)
            ring_copy(1, 1 - k, k, c).start()
            forward(1, k, k, c)

        each(pieces, second)

    def later(step, carry):
        def piece(index):
            k, c = index // pieces, lax.rem(index, pieces)
            compute(step, k, c)
            for way in range(2):
                forward(step, way, k, c)

        each(2 * pieces, piece)
        return carry

    lax.fori_loop(2, half, later, 0)

    for k in range(2):
        row = lax.broadcasted_iota(jnp.int32, (rc, cap), 0) + me * rc
        column = lax.broadcasted_iota(jnp.int32, (rc, cap), 1)
        keep = (row < dims_s[k, 0]) & (column < dims_s[k, 1])
        for c in range(pieces):
            total = part[0, 1, k, :, c * wide:(c + 1) * wide]
            for way in range(2):
                ring_copy(half - 1, way, k, c).wait_recv()
                total = total + arrived[half - 1, way, k, :, c * wide:(c + 1) * wide]
            for p in range(wide // cap):
                out[k, :, c * (wide // cap) + p, :] = jnp.where(keep, total[:, p * cap:(p + 1) * cap], 0.0)

    def drain(c):
        for k in range(2):
            ring_copy(0, k, k, c).wait_send()
            for way in range(2):
                each(half - 1, lambda step: ring_copy(step + 1, way, k, c).wait_send())

    each(pieces, drain)
    each(blocks, lambda cb: [halo_block(side, cb).wait_send() for side in (0, 1)])


def body(theta, block_dims, pair_mask, term_charge, left_env, right_env, site_one, site_two):
    sectors, cap, pairs, _ = theta.shape
    terms = left_env.shape[0]
    half = lax.axis_size("mpo") // 2
    rc = cap // (2 * half)
    anywhere = pl.BlockSpec(memory_space=pl.ANY)
    vmem = pl.BlockSpec(memory_space=pltpu.VMEM)
    smem = pl.BlockSpec(memory_space=pltpu.SMEM)
    return pl.pallas_call(
        kernel,
        out_shape=jax.ShapeDtypeStruct((sectors, rc, pairs, cap), F32),
        in_specs=[anywhere] * 3 + [smem] * 5,
        out_specs=vmem,
        scratch_shapes=[
            pltpu.VMEM((sectors, cap * pairs, cap), F32),
            pltpu.VMEM((2, cap * pairs, cap), F32),
            pltpu.VMEM(left_env.shape, F32),
            pltpu.VMEM(right_env.shape, F32),
            pltpu.VMEM((2, 8, cap), F32),
            pltpu.VMEM((2, 8, cap), F32),
            pltpu.VMEM((4, 8, cap), F32),
            pltpu.VMEM((4, cap // CB, pairs * CB, 2 * cap), BF16),
            pltpu.VMEM((2 * terms, 2 * cap, 2 * cap), BF16),
            pltpu.VMEM((2 * terms, 2 * cap, pairs * cap), BF16),
            pltpu.VMEM((half, 2, terms, 4 * rc, 2 * cap), BF16),
            pltpu.VMEM((half, 2, 2, rc, pairs * cap), F32),
            pltpu.VMEM((half, 2, 2, rc, pairs * cap), F32),
            pltpu.SemaphoreType.DMA((3,)),
            pltpu.SemaphoreType.DMA((cap // CB + 1, 2)),
            pltpu.SemaphoreType.DMA((cap // CB + 1, 2)),
            pltpu.SemaphoreType.DMA((half, 2, 2, pairs * cap // WIDE)),
            pltpu.SemaphoreType.DMA((half, 2, 2, pairs * cap // WIDE)),
        ],
        compiler_params=pltpu.CompilerParams(
            collective_id=0, has_side_effects=True, vmem_limit_bytes=60 * 2**20
        ),
    )(
        theta.reshape(sectors, cap * pairs, cap), left_env, right_env, block_dims, term_charge,
        pair_mask.T, jnp.transpose(site_one, (1, 2, 0)), jnp.transpose(site_two, (1, 2, 0)),
    )


def solution(mesh):
    placed = (
        P("blk", None, None, None),
        P("blk", None),
        P(None, "blk"),
        P(),
        P("mpo", "blk", None, None),
        P("mpo", "blk", None, None),
        P(),
        P(),
    )
    return jax.shard_map(
        body, mesh=mesh, in_specs=placed, out_specs=P("blk", "mpo", None, None), check_vma=False
    )
```

time: 89.4 us -> 69.2 us (0.77)
  the two profiles are of different devices: /device:TPU:16 before, /device:TPU:32 now
where the time goes in v2:
time: 69.2 us; the launch traced here: 69 us
  Pallas kernels  67.4 us (97%)
  local copies, waits for them, and re-layouts  1.57 us (2%)
    pallas_call x1, Pallas kernels, body(): pl.pallas_call(kernel, out_shape=jax.ShapeDtypeStruct((sectors, rc, pairs...  67.4 us
    unnamed x1, local copies, waits for them, and re-layouts  1.57 us

profile of v2, /device:TPU:32, one launch (start us, length us, event | category | flops | bytes accessed | tf_op | source)
XLA Modules:
  0.0 69.0 jit_solution(13989609263027398121)
XLA Ops:
  0.0 67.4 %shard_map.82 = f32[2,8,16,128]{3,2,1,0:T(8,128)} custom-call(f32[2,2048,128]{2,1,0:T(8,128)} %bitcast.4, f32[6,2,128,128]{3,2,1,0:T(8,128)} %left.1, f32[6,2,128,128]{3,2,1,0:T(8,128)} %right.1, s32[2,2]{1,0:T(2,128)} %dims_s.1, s32[96]{0:T(128)} %charge.1, s32[2,96]{1,0:T(2,128)} %bitcast.7, f32[4,4,96]{2,1,0:T(4,128)} %bitcast.5, f32[4,4,96]{2,1,0:T(4,128)} %bitcast.6), custom_call_target="tpu_custom_call" | custom-call | tf_op jit(solution)/shard_map/pallas_call | solution.py:268
  67.4 1.6 %copy.10 = f32[2,8,16,128]{3,2,1,0:T(8,128)} copy(f32[2,8,16,128]{3,2,1,0:T(8,128)} %shard_map.82) | data formatting | bytes 262144

commit v3 on v2

--- a/solution.py
+++ b/solution.py
@@ -123,8 +123,8 @@
         k = jnp.where(q == 1, 0, 1)
         return terms + w, w, k, k + 1 - q
 
-    def each(count, task):
-        lax.fori_loop(0, count, lambda index, carry: (task(index), carry)[1], 0)
+    def each(count, task, unroll=1):
+        lax.fori_loop(0, count, lambda index, carry: (task(index), carry)[1], 0, unroll=unroll)
 
     dims_all[1] = dims_v[0]
     dims_all[2] = dims_v[1]
@@ -134,7 +134,7 @@
     each(terms, lambda w: weigh(*near(w)))
 
     def near_term(w):
-        each(blocks, lambda cb: apply_right(*near(w), cb))
+        each(blocks, lambda cb: apply_right(*near(w), cb), 4)
 
     each(terms, near_term)
 
@@ -146,7 +146,7 @@
 
     local[1].wait()
 
-    def rotate(g, carry):
+    def rotate(g):
         ahead = pl.multiple_of(lax.rem(me + half - g, n) * rc, rc)
         behind = pl.multiple_of(jnp.where(g == 0, me, lax.rem(me + n - half + g, n)) * rc, rc)
         for w in range(terms):
@@ -164,15 +164,12 @@
                     ],
                     axis=0,
                 )
-        return carry
-
-    lax.fori_loop(0, half, rotate, 0)
 
     def far_block(cb):
         for side, source in ((0, 0), (1, 3)):
             halo_block(side, cb).wait_recv()
             prepare(source, halo_v, side, cb)
-        each(terms, lambda w: apply_right(*far(w), cb))
+        each(terms, lambda w: apply_right(*far(w), cb), 3)
 
     each(blocks, far_block)
 
@@ -207,6 +204,7 @@
         part[step, way, k, :, columns(c)] += arrived[step - 1, way, k, :, columns(c)]
         ring_copy(step, way, k, c).start()
 
+    rotate(0)
     for k in range(2):
 
         def farthest(c):
@@ -214,6 +212,7 @@
             ring_copy(0, k, k, c).start()
 
         each(pieces, farthest)
+    rotate(1)
     for k in range(2):
 
         def second(c):
@@ -224,6 +223,8 @@
         each(pieces, second)
 
     def later(step, carry):
+        rotate(step)
+
         def piece(index):
             k, c = index // pieces, lax.rem(index, pieces)
             compute(step, k, c)

time: 69.2 us -> 64 us (0.925)
  Pallas kernels: 67.4 us -> 62.2 us
    pallas_call x1, Pallas kernels: 67.4 us -> 62.2 us  [body(): pl.pallas_call(kernel, out_shape=jax.ShapeDtypeStruct((sectors, rc, pairs...]
where the time goes in v3:
time: 64 us; the launch traced here: 63.8 us
  Pallas kernels  62.2 us (97%)
  local copies, waits for them, and re-layouts  1.57 us (2%)
    pallas_call x1, Pallas kernels, body(): pl.pallas_call(kernel, out_shape=jax.ShapeDtypeStruct((sectors, rc, pairs...  62.2 us
    unnamed x1, local copies, waits for them, and re-layouts  1.57 us

profile of v3, /device:TPU:32, one launch (start us, length us, event | category | flops | bytes accessed | tf_op | source)
XLA Modules:
  0.0 63.8 jit_solution(13066098787414059398)
XLA Ops:
  0.0 62.2 %shard_map.82 = f32[2,8,16,128]{3,2,1,0:T(8,128)} custom-call(f32[2,2048,128]{2,1,0:T(8,128)} %bitcast.4, f32[6,2,128,128]{3,2,1,0:T(8,128)} %left.1, f32[6,2,128,128]{3,2,1,0:T(8,128)} %right.1, s32[2,2]{1,0:T(2,128)} %dims_s.1, s32[96]{0:T(128)} %charge.1, s32[2,96]{1,0:T(2,128)} %bitcast.7, f32[4,4,96]{2,1,0:T(4,128)} %bitcast.5, f32[4,4,96]{2,1,0:T(4,128)} %bitcast.6), custom_call_target="tpu_custom_call" | custom-call | tf_op jit(solution)/shard_map/pallas_call | solution.py:269
  62.2 1.6 %copy.10 = f32[2,8,16,128]{3,2,1,0:T(8,128)} copy(f32[2,8,16,128]{3,2,1,0:T(8,128)} %shard_map.82) | data formatting | bytes 262144

commit v4 on v3

--- a/solution.py
+++ b/solution.py
@@ -10,7 +10,7 @@
 MESH = pl.DeviceIdType.MESH
 F32 = jnp.float32
 BF16 = jnp.bfloat16
-CB = 32
+CB = 16
 RB = 16
 WIDE = 1024
 
@@ -134,7 +134,7 @@
     each(terms, lambda w: weigh(*near(w)))
 
     def near_term(w):
-        each(blocks, lambda cb: apply_right(*near(w), cb), 4)
+        each(blocks, lambda cb: apply_right(*near(w), cb), 8)
 
     each(terms, near_term)
 
@@ -169,7 +169,7 @@
         for side, source in ((0, 0), (1, 3)):
             halo_block(side, cb).wait_recv()
             prepare(source, halo_v, side, cb)
-        each(terms, lambda w: apply_right(*far(w), cb), 3)
+        each(terms, lambda w: apply_right(*far(w), cb), 6)
 
     each(blocks, far_block)
 

time: 64 us -> 63 us (0.984)
  Pallas kernels: 62.2 us -> 61.3 us
    pallas_call x1, Pallas kernels: 62.2 us -> 61.3 us  [body(): pl.pallas_call(kernel, out_shape=jax.ShapeDtypeStruct((sectors, rc, pairs...]
where the time goes in v4:
time: 63 us; the launch traced here: 62.9 us
  Pallas kernels  61.3 us (97%)
  local copies, waits for them, and re-layouts  1.57 us (2%)
    pallas_call x1, Pallas kernels, body(): pl.pallas_call(kernel, out_shape=jax.ShapeDtypeStruct((sectors, rc, pairs...  61.3 us
    unnamed x1, local copies, waits for them, and re-layouts  1.57 us

profile of v4, /device:TPU:32, one launch (start us, length us, event | category | flops | bytes accessed | tf_op | source)
XLA Modules:
  0.0 62.9 jit_solution(12087699370261779381)
XLA Ops:
  0.0 61.3 %shard_map.82 = f32[2,8,16,128]{3,2,1,0:T(8,128)} custom-call(f32[2,2048,128]{2,1,0:T(8,128)} %bitcast.4, f32[6,2,128,128]{3,2,1,0:T(8,128)} %left.1, f32[6,2,128,128]{3,2,1,0:T(8,128)} %right.1, s32[2,2]{1,0:T(2,128)} %dims_s.1, s32[96]{0:T(128)} %charge.1, s32[2,96]{1,0:T(2,128)} %bitcast.7, f32[4,4,96]{2,1,0:T(4,128)} %bitcast.5, f32[4,4,96]{2,1,0:T(4,128)} %bitcast.6), custom_call_target="tpu_custom_call" | custom-call | tf_op jit(solution)/shard_map/pallas_call | solution.py:269
  61.3 1.6 %copy.10 = f32[2,8,16,128]{3,2,1,0:T(8,128)} copy(f32[2,8,16,128]{3,2,1,0:T(8,128)} %shard_map.82) | data formatting | bytes 262144

commit v5 on v4

--- a/solution.py
+++ b/solution.py
@@ -191,6 +191,19 @@
         part[g, 0, k, :, columns(c)] = total[:rc]
         part[g, 1, k, :, columns(c)] = total[rc:]
 
+    def compute_two(g, k, c):
+        total = jnp.zeros((8 * rc, wide), F32)
+        for w in range(terms):
+            q = charge[w0 + w]
+            slot = w + jnp.where((q == 1) == (k == 1), 0, terms)
+            both = jnp.concatenate([rows[g, k, w], rows[g + 1, k, w]], axis=0)
+            total += jnp.dot(both, mixed[slot, :, columns(c)], preferred_element_type=F32)
+        for step in range(2):
+            mine = total[step * 4 * rc:(step + 1) * 4 * rc]
+            mine = mine[:2 * rc] + mine[2 * rc:]
+            part[g + step, 0, k, :, columns(c)] = mine[:rc]
+            part[g + step, 1, k, :, columns(c)] = mine[rc:]
+
     def ring_copy(step, way, k, c):
         row = 0 if isinstance(step, int) and step == 0 else way
         return pltpu.make_async_remote_copy(
@@ -222,19 +235,27 @@
 
         each(pieces, second)
 
-    def later(step, carry):
+    def later(index, carry):
+        step = 2 * index
         rotate(step)
+        rotate(step + 1)
 
         def piece(index):
             k, c = index // pieces, lax.rem(index, pieces)
-            compute(step, k, c)
+            compute_two(step, k, c)
             for way in range(2):
                 forward(step, way, k, c)
 
+        def passed(index):
+            for way in range(2):
+                forward(step + 1, way, index // pieces, lax.rem(index, pieces))
+
         each(2 * pieces, piece)
+        each(2 * pieces, passed)
         return carry
 
-    lax.fori_loop(2, half, later, 0)
+    assert half % 2 == 0
+    lax.fori_loop(1, half // 2, later, 0)
 
     for k in range(2):
         row = lax.broadcasted_iota(jnp.int32, (rc, cap), 0) + me * rc

time: 63 us -> 63.2 us (level)
  no operation moved by 1% of the time
where the time goes in v5:
time: 63.2 us; the launch traced here: 63 us
  Pallas kernels  61.4 us (97%)
  local copies, waits for them, and re-layouts  1.57 us (2%)
    pallas_call x1, Pallas kernels, body(): pl.pallas_call(kernel, out_shape=jax.ShapeDtypeStruct((sectors, rc, pairs...  61.4 us
    unnamed x1, local copies, waits for them, and re-layouts  1.57 us

profile of v5, /device:TPU:32, one launch (start us, length us, event | category | flops | bytes accessed | tf_op | source)
XLA Modules:
  0.0 63.0 jit_solution(12380365908442544378)
XLA Ops:
  0.0 61.4 %shard_map.82 = f32[2,8,16,128]{3,2,1,0:T(8,128)} custom-call(f32[2,2048,128]{2,1,0:T(8,128)} %bitcast.4, f32[6,2,128,128]{3,2,1,0:T(8,128)} %left.1, f32[6,2,128,128]{3,2,1,0:T(8,128)} %right.1, s32[2,2]{1,0:T(2,128)} %dims_s.1, s32[96]{0:T(128)} %charge.1, s32[2,96]{1,0:T(2,128)} %bitcast.7, f32[4,4,96]{2,1,0:T(4,128)} %bitcast.5, f32[4,4,96]{2,1,0:T(4,128)} %bitcast.6), custom_call_target="tpu_custom_call" | custom-call | tf_op jit(solution)/shard_map/pallas_call | solution.py:290
  61.4 1.6 %copy.10 = f32[2,8,16,128]{3,2,1,0:T(8,128)} copy(f32[2,8,16,128]{3,2,1,0:T(8,128)} %shard_map.82) | data formatting | bytes 262144
